TPU v7x, 512 devices: a whole 4x8x8 slice. The times are simulated.
512 devices in a mesh: seq: 32 (over z_lo, y, core), head: 16 (over x, z_hi).
Axes of the slice: x: 4, y: 8, z: 8 (z_hi: 4, z_lo: 2; z = z_hi * 2 + z_lo), core: 2. Of those that a mesh axis runs over, the one named last changes fastest.
Arguments:
- q_nope: bfloat16 [3072, 16384], P('seq', 'head'), may hold values from -6 to 6
- q_rope: bfloat16 [3072, 8192], P('seq', 'head'), may hold values from -48 to 48
- w_uk: bfloat16 [128, 128, 512], P('head'), may hold values from -0.5 to 0.5
- w_uv: bfloat16 [128, 512, 128], P('head'), may hold values from -0.25 to 0.25
- w_value: float32 [16384], P('head'), may hold values from -0.1875 to 0.1875
- kv_cache: bfloat16 [4096, 576], P('seq'), may hold values from -8 to 8
- cutoffs: int32 [3072], P('seq'), may hold values from 1 to 4096, as said below
Outputs:
- attn: bfloat16 [3072, 16384], P('seq', 'head')
- value: float32 [3072], P('seq')
Inputs may be any that keep to these rules, and one draw needn't show every extreme that they name: `cutoffs`: every row sees at least the first event; some row sees the whole history and some row only the first event.
All inputs are finite; a program needn't handle non-finite values.
Results may differ from a plain program's by a relative error of at most 0.014.
Values may be sent and summed in bfloat16 or wider, within the bound.
A program may use at most 64 MiB of HBM per device.

v0:
```python
import jax
import jax.numpy as jnp
from jax import lax
from jax.sharding import PartitionSpec as P

softmax_scale = (128.0 + 64.0) ** (-0.5)


def on_device(q_nope, q_rope, w_uk, w_uv, w_value, kv_cache, cutoffs):
    rows = q_nope.shape[0]
    heads = w_uk.shape[0]
    latent = w_uk.shape[2]
    nope_rows = q_nope.reshape(rows, heads, w_uk.shape[1])
    q_lat = jnp.einsum("rhn,hnc->rhc", nope_rows, w_uk, preferred_element_type=jnp.float32).astype(
        jnp.bfloat16
    )
    q_all = jnp.concatenate([q_lat, q_rope.reshape(rows, heads, -1)], axis=2)
    piece = lax.all_gather(kv_cache, "seq", axis=0, tiled=True)
    running = jnp.full((rows, heads), -1e30, jnp.float32)
    count = piece.shape[0]
    score = (
        jnp.einsum("rhc,ec->rhe", q_all, piece, preferred_element_type=jnp.float32) * softmax_scale
    )
    index = jnp.arange(count, dtype=jnp.int32)
    keep = index[None, None, :] < cutoffs[:, None, None]
    score = jnp.where(keep, score, -jnp.inf)
    newest = jnp.maximum(running, jnp.max(score, axis=2))
    weight = jnp.exp(score - newest[:, :, None])
    total = jnp.sum(weight, axis=2)
    update = jnp.einsum(
        "rhe,ec->rhc",
        weight.astype(jnp.bfloat16),
        piece[:, :latent],
        preferred_element_type=jnp.float32,
    )
    accum = update
    running, total, accum = (newest, total, accum)
    o_lat = (accum / total[:, :, None]).astype(jnp.bfloat16)
    attn = jnp.einsum("rhc,hcv->rhv", o_lat, w_uv, preferred_element_type=jnp.float32).astype(
        jnp.bfloat16
    )
    attn = attn.reshape(rows, -1)
    partial_score = jnp.sum(attn.astype(jnp.float32) * w_value[None, :], axis=1)
    value = lax.psum(partial_score, "head")
    return (attn, value)


def solution(mesh):
    placed = (
        P("seq", "head"),
        P("seq", "head"),
        P("head", None, None),
        P("head", None, None),
        P("head"),
        P("seq", None),
        P("seq"),
    )
    return jax.shard_map(
        on_device,
        mesh=mesh,
        in_specs=placed,
        out_specs=(P("seq", "head"), P("seq")),
        check_vma=False,
    )
```

profile of v0, /device:TPU:16, one launch (start us, length us, event | category | flops | bytes accessed | tf_op | source)
XLA Modules:
  0.0 163.2 jit_solution(10106467120380042580)
XLA Ops:
  7.2 0.0 copy-start
  7.2 0.0 all-gather.2.cloned.1.call-start
  7.2 0.7 all-gather.2.cloned.1.call-update
  7.9 1.0 copy.13
  8.9 0.2 copy.14
  9.1 0.0 copy-done
  9.1 1.3 fusion.11
  10.4 0.1 pad_maximum_fusion
  10.5 1.0 iota_compare_fusion
  11.4 79.9 %all-gather.2.cloned.1.call-done = bf16[4096,576]{0,1:T(8,128)(2,1)} async-done(((bf16[128,576]{0,1:T(8,128)(2,1)}), bf16[4096,576]{0,1:T(8,128)(2,1)}) %all-gather.2.cloned.1.call-update) | async-done | bytes 4718608 | tf_op jit(solution)/shard_map/all_gather | solution.py:18
  91.3 8.0 %fusion = (f32[96,8]{1,0:T(8,128)S(1)}, f32[96,8,4096]{2,1,0:T(8,128)S(1)}) fusion(pred[96,4096]{1,0:T(8,128)(4,1)S(1)} %iota_compare_fusion, bf16[4096,576]{0,1:T(8,128)(2,1)} %all-gather.2.cloned.1.call-done, bf16[96,8,576]{2,0,1:T(8,128)(2,1)S(1)} %pad_maximum_fusion), kind=kOutput, calls=%fused_computation.2 | convolution fusion | flops 3633315072 | bytes 18582528 | tf_op jit(solution)/shard_map/rhc,ec->rhe/dot_general | solution.py:22
  99.3 3.9 %fusion.1 = f32[96,8]{1,0:T(8,128)S(1)} fusion(f32[96,8,4096]{2,1,0:T(8,128)S(1)} %get-tuple-element.3, f32[96,8]{1,0:T(8,128)S(1)} %broadcast_maximum_fusion, pred[96,4096]{1,0:T(8,128)(4,1)S(1)} %iota_compare_fusion), kind=kLoop, calls=%fused_computation.3 | loop fusion | flops 12582144 | bytes 12982272 | tf_op jit(solution)/shard_map/reduce_sum | solution.py:29
  103.2 0.0 copy-start.1
  103.2 0.0 copy-start.2
  103.2 6.1 %divide_convert_fusion = bf16[96,8,512]{2,1,0:T(8,128)(2,1)S(1)} fusion(bf16[4096,576]{0,1:T(8,128)(2,1)} %all-gather.2.cloned.1.call-done, f32[96,8,4096]{2,1,0:T(8,128)S(1)} %get-tuple-element.3, f32[96,8]{1,0:T(8,128)S(1)} %broadcast_maximum_fusion, pred[96,4096]{1,0:T(8,128)(4,1)S(1)} %iota_compare_fusion, f32[96,8]{1,0:T(8,128)S(1)} %fusion.1), kind=kOutput, calls=%fused_computation.13 | convolution fusion | flops 3234594816 | bytes 17963008 | tf_op jit(solution)/shard_map/rhe,ec->rhc/dot_general | solution.py:30
  109.3 0.0 copy-done.1
  109.3 0.0 copy-done.2
  109.3 0.7 multiply_reduce_fusion
  110.0 45.7 %psum.7 = f32[96]{0:T(128)} all-reduce(f32[96]{0:T(128)S(1)} %get-tuple-element.4), channel_id=1, replica_groups=mesh['seq'=32,'head'=16] {'head'}, use_global_device_ids=true, to_apply=%region_3.4 | all-reduce | flops 96 | bytes 768 | tf_op jit(solution)/shard_map/psum | solution.py:44
  155.7 0.7 copy_bitcast_fusion
  (1 shorter events, 0.0 us)
Async XLA Ops:
  7.2 1.9 %copy-start = (bf16[8,128,512]{2,1,0:T(8,128)(2,1)S(1)}, bf16[8,128,512]{2,1,0:T(8,128)(2,1)}, u32[]{:S(2)}) copy-start(bf16[8,128,512]{2,1,0:T(8,128)(2,1)} %param.9) | copy-start | bytes 3145732
  7.2 84.1 %all-gather.2.cloned.1.call-start = ((), (), s32[]{:S(2)}) async-start(), calls=%async_computation | async-start | bytes 4866048 | tf_op jit(solution)/shard_map/all_gather | solution.py:18
  103.2 6.1 %copy-start.1 = (bf16[8,512,128]{2,1,0:T(8,128)(2,1)S(1)}, bf16[8,512,128]{2,1,0:T(8,128)(2,1)}, u32[]{:S(2)}) copy-start(bf16[8,512,128]{2,1,0:T(8,128)(2,1)} %param.10) | copy-start | bytes 3145732
  103.2 6.1 %copy-start.2 = (f32[1024]{0:T(1024)S(1)}, f32[1024]{0:T(1024)}, u32[]{:S(2)}) copy-start(f32[1024]{0:T(1024)} %param.11) | copy-start | bytes 12292
Sparse Core Ops, SparseCore 0:
  10.1 81.1 all-gather.1
where the time goes:
time: 163 us
  waiting for transfers between devices  80.5 us (49%)
  blocking collectives  45.7 us (28%)
  matrix products  16 us (10%)
  between operations  14.1 us (9%)
  other arithmetic  4.93 us (3%)
  local copies, waits for them, and re-layouts  1.87 us (1%)
    all_gather x1, waiting for transfers between devices, on_device(): piece = lax.all_gather(kv_cache, 'seq', axis=0, tiled=True)  79.9 us
    psum x1, blocking collectives, on_device(): value = lax.psum(partial_score, 'head')  45.7 us
    dot_general x1, matrix products, on_device(): jnp.einsum('rhc,ec->rhe', q_all, piece, preferred_element_type=jnp.float32)  7.95 us
    dot_general x1, matrix products, on_device(): jnp.einsum('rhe,ec->rhc', weight.astype(jnp.bfloat16), piece[:, :latent],...  6.09 us
    reduce_sum x1, other arithmetic, on_device(): total = jnp.sum(weight, axis=2)  3.89 us
  transfers between devices with their start and end apart: 1, of which 1 were waited for; matrix products, arithmetic and copies ran while one was open for 2% of the time, Pallas kernels for 0%

commit v1 on v0

v1 whole, which is shorter than its diff:
```python
import jax
import jax.numpy as jnp
from jax import lax
from jax.experimental import pallas as pl
from jax.experimental.pallas import tpu as pltpu
from jax.sharding import PartitionSpec as P

MESH = pl.DeviceIdType.MESH
softmax_scale = (128.0 + 64.0) ** (-0.5)
exp2_scale = softmax_scale * 1.4426950408889634
HIDDEN = -1e30
Y, Z_HI, X = 8, 4, 4
SHARD = 128
HALF = 64
CHIP = 2 * SHARD
BLOCKS = 2


def chip_slot(plane, away):
    if away == 0:
        return plane
    if away == 4:
        return 14 + plane
    if away < 4:
        return 2 + (away - 1) * 4 + plane * 2
    return 2 + (7 - away) * 4 + plane * 2 + 1


def kernel(
    qn, qr, w_uk, w_uv, w_value, kv, cut, attn, value,
    held, q_all, accum, top, total, x_sums, z_sums,
    y_send, y_recv, z_send, z_recv, c_send, c_recv, v_send, v_recv, own_sem,
):
    rows = qn.shape[0]
    heads, _, latent = w_uk.shape
    rope = qr.shape[1] // heads
    seq, head = lax.axis_index("seq"), lax.axis_index("head")
    core = lax.rem(seq, 2)
    y = lax.rem(lax.div(seq, 2), Y)
    z_lo = lax.div(seq, 2 * Y)
    x, z_hi = lax.div(head, Z_HI), lax.rem(head, Z_HI)

    def at_y(step):
        return ((z_lo * Y + lax.rem(y + step + Y, Y)) * 2 + core, head)

    other_plane = seq + (1 - 2 * z_lo) * 2 * Y
    z_up = (other_plane, x * Z_HI + lax.rem(z_hi + z_lo, Z_HI))
    z_down = (other_plane, x * Z_HI + lax.rem(z_hi + z_lo + Z_HI - 1, Z_HI))
    twin = (seq + 1 - 2 * core, head)
    y_to = (at_y(1), at_y(-1))
    z_to = (z_up, z_down)
    x_peers = [(seq, lax.rem(x + k, X) * Z_HI + z_hi) for k in range(1, X)]
    z_peers = [(seq, x * Z_HI + lax.rem(z_hi + k, Z_HI)) for k in range(1, Z_HI)]

    barrier = pltpu.get_barrier_semaphore()
    greeted = [*y_to, *z_to, twin, *x_peers, *z_peers]
    for device in greeted:
        pl.semaphore_signal(barrier, inc=1, device_id=device, device_id_type=MESH)

    def place(slot, half=None):
        start = slot * CHIP + core * SHARD
        if half is None:
            return held.at[pl.ds(pl.multiple_of(start, SHARD), SHARD)]
        return held.at[pl.ds(pl.multiple_of(start + half * HALF, HALF), HALF)]

    def own(half):
        return kv.at[pl.ds(half * HALF, HALF)]

    def half_of(stream, unit):
        return unit % 2 if stream == 0 else 1 - unit % 2

    def away(stream, steps):
        return steps if stream == 0 else (Y - steps) % Y

    def y_copy(stream, unit):
        steps, half = unit // 2, half_of(stream, unit)
        source = own(half) if steps == 0 else place(chip_slot(0, away(stream, steps)), half)
        return pltpu.make_async_remote_copy(
            src_ref=source,
            dst_ref=place(chip_slot(0, away(stream, steps + 1)), half),
            send_sem=y_send.at[stream, unit],
            recv_sem=y_recv.at[stream, unit],
            device_id=y_to[stream],
            device_id_type=MESH,
        )

    def z_copy(stream, unit):
        if unit == 0:
            steps, half = 0, stream
            source = own(half)
        else:
            steps, half = (unit - 1) // 2 + 1, half_of(stream, unit - 1)
            source = place(chip_slot(0, away(stream, steps)), half)
        return pltpu.make_async_remote_copy(
            src_ref=source,
            dst_ref=place(chip_slot(1, away(stream, steps)), half),
            send_sem=z_send.at[stream, unit],
            recv_sem=z_recv.at[stream, unit],
            device_id=z_to[stream],
            device_id_type=MESH,
        )

    def twin_copy(index):
        if index == 0:
            source, target = kv, place(chip_slot(0, 0))
        else:
            if index < 15:
                stream, unit = (index - 1) % 2, (index - 1) // 2
                slot, half = chip_slot(0, away(stream, unit // 2 + 1)), half_of(stream, unit)
            else:
                stream, unit = (index - 15) % 2, (index - 15) // 2
                if unit == 0:
                    slot, half = chip_slot(1, 0), stream
                else:
                    slot = chip_slot(1, away(stream, (unit - 1) // 2 + 1))
                    half = half_of(stream, unit - 1)
            source = target = place(slot, half)
        return pltpu.make_async_remote_copy(
            src_ref=source,
            dst_ref=target,
            send_sem=c_send.at[index],
            recv_sem=c_recv.at[index],
            device_id=twin,
            device_id_type=MESH,
        )

    def from_y(unit):
        for stream in range(2):
            y_copy(stream, unit).wait_recv()
            if unit + 2 < 7:
                y_copy(stream, unit + 2).start()
            z_copy(stream, unit + 1).start()
            twin_copy(1 + unit * 2 + stream).start()

    def from_z(unit):
        for stream in range(2):
            z_copy(stream, unit).wait_recv()
            twin_copy(15 + unit * 2 + stream).start()

    def from_twin(*indices):
        for index in indices:
            twin_copy(index).wait_recv()

    keep_own = pltpu.make_async_copy(kv, place(chip_slot(0, 0)), own_sem)

    def first_event(plane, steps):
        z_at = lax.rem(z_lo + plane, 2)
        return (z_at * Y + lax.rem(y - steps + Y, Y)) * CHIP

    def attend(pair):
        if pair == 0:
            chips = ((0, 0), (1, 0))
        elif pair == 7:
            chips = ((0, 4), (1, 4))
        else:
            steps, plane = (pair - 1) // 2 + 1, (pair - 1) % 2
            chips = ((plane, steps), (plane, Y - steps))
        first, second = first_event(*chips[0]), first_event(*chips[1])
        size = 2 * CHIP
        column = lax.broadcasted_iota(jnp.int32, (rows, size), 1)
        event = column + jnp.where(column < CHIP, first, second - CHIP)
        bias = jnp.where(event < cut[...], 0.0, HIDDEN)
        block = held[pl.ds(pair * size, size), :]
        per = heads // BLOCKS
        for part in range(BLOCKS):
            span = pl.ds(part * per * rows, per * rows)
            score = lax.dot_general(
                q_all[span, :], block, (((1,), (1,)), ((), ())), preferred_element_type=jnp.float32
            )
            weights, scales = [], []
            for h in range(per):
                mine = pl.ds((part * per + h) * rows, rows)
                s = score[h * rows : (h + 1) * rows, :] + bias
                newest = jnp.max(s, axis=1, keepdims=True)
                if pair > 0:
                    newest = jnp.maximum(newest, top[mine, 0:1])
                    scale = jnp.exp2((top[mine, 0:1] - newest) * exp2_scale)
                    scales.append(scale)
                w = jnp.exp2((s - newest) * exp2_scale)
                added = sum(w[:, k : k + 128] for k in range(128, size, 128)) + w[:, :128]
                total[mine, :] = added if pair == 0 else total[mine, :] * scale + added
                top[mine, :] = jnp.broadcast_to(newest, (rows, 128))
                weights.append(w.astype(jnp.bfloat16))
            update = jnp.dot(
                jnp.concatenate(weights, axis=0), block[:, :latent], preferred_element_type=jnp.float32
            )
            if pair == 0:
                accum[span, :] = update
            else:
                accum[span, :] = accum[span, :] * jnp.concatenate(scales, axis=0) + update

    for h in range(heads):
        mine = pl.ds(h * rows, rows)
        q_lat = jnp.dot(qn[:, h * 128 : (h + 1) * 128], w_uk[h], preferred_element_type=jnp.float32)
        q_all[mine, :latent] = q_lat.astype(jnp.bfloat16)
        q_all[mine, latent:] = qr[:, h * rope : (h + 1) * rope]

    pl.semaphore_wait(barrier, len(greeted))
    for unit in range(2):
        for stream in range(2):
            y_copy(stream, unit).start()
            if unit == 0:
                z_copy(stream, 0).start()
    twin_copy(0).start()
    keep_own.start()

    from_y(0)
    from_z(0)
    from_y(1)
    keep_own.wait()
    from_twin(0, 15, 16)
    attend(0)
    from_y(2)
    from_z(1)
    from_z(2)
    from_twin(1, 2, 3, 4)
    attend(1)
    from_y(3)
    from_twin(17, 18, 19, 20)
    attend(2)
    from_y(4)
    from_z(3)
    from_z(4)
    from_twin(5, 6, 7, 8)
    attend(3)
    from_y(5)
    from_twin(21, 22, 23, 24)
    attend(4)
    from_y(6)
    from_z(5)
    from_z(6)
    from_twin(9, 10, 11, 12)
    attend(5)
    from_z(7)
    from_twin(25, 26, 27, 28)
    attend(6)
    from_twin(13, 14, 29, 30)
    attend(7)

    share = jnp.zeros((rows, 128), jnp.float32)
    for h in range(heads):
        mine = pl.ds(h * rows, rows)
        inverse = 1.0 / jnp.sum(total[mine, :], axis=1, keepdims=True)
        o_lat = (accum[mine, :] * inverse).astype(jnp.bfloat16)
        out = jnp.dot(o_lat, w_uv[h], preferred_element_type=jnp.float32).astype(jnp.bfloat16)
        attn[:, h * 128 : (h + 1) * 128] = out
        share = share + out.astype(jnp.float32) * w_value[h : h + 1, :]
    partial = lax.dot_general(
        jnp.ones((8, 128), jnp.float32), share, (((1,), (1,)), ((), ())),
        precision=lax.Precision.HIGHEST, preferred_element_type=jnp.float32,
    )

    def exchange(stage, sums, peers, place_here, count, mine):
        sums[0, :, :rows] = mine
        copies = [
            pltpu.make_async_remote_copy(
                src_ref=sums.at[0],
                dst_ref=sums.at[k],
                send_sem=v_send.at[stage, k],
                recv_sem=v_recv.at[stage, k],
                device_id=peers[k - 1],
                device_id_type=MESH,
            )
            for k in range(1, count)
        ]
        for copy in copies:
            copy.start()
        for copy in copies:
            copy.wait()
        result = sums[place_here, :, :rows]
        for j in range(1, count):
            result = result + sums[lax.rem(place_here - j + count, count), :, :rows]
        return result

    along_x = exchange(0, x_sums, x_peers, x, X, partial)
    value[...] = exchange(1, z_sums, z_peers, z_hi, Z_HI, along_x)

    for stream in range(2):
        for unit in range(7):
            y_copy(stream, unit).wait_send()
        for unit in range(8):
            z_copy(stream, unit).wait_send()
    for index in range(31):
        twin_copy(index).wait_send()


def on_device(q_nope, q_rope, w_uk, w_uv, w_value, kv_cache, cutoffs):
    rows = q_nope.shape[0]
    heads, _, latent = w_uk.shape
    depth = kv_cache.shape[1]
    vmem = pl.BlockSpec(memory_space=pltpu.VMEM)
    dma = pltpu.SemaphoreType.DMA
    attn, value = pl.pallas_call(
        kernel,
        out_shape=(
            jax.ShapeDtypeStruct((rows, q_nope.shape[1]), jnp.bfloat16),
            jax.ShapeDtypeStruct((8, rows), jnp.float32),
        ),
        in_specs=[vmem] * 7,
        out_specs=(vmem, vmem),
        scratch_shapes=[
            pltpu.VMEM((16 * CHIP, depth), jnp.bfloat16),
            pltpu.VMEM((heads * rows, depth), jnp.bfloat16),
            pltpu.VMEM((heads * rows, latent), jnp.float32),
            pltpu.VMEM((heads * rows, 128), jnp.float32),
            pltpu.VMEM((heads * rows, 128), jnp.float32),
            pltpu.VMEM((X, 8, 128), jnp.float32),
            pltpu.VMEM((Z_HI, 8, 128), jnp.float32),
            dma((2, 7)), dma((2, 7)), dma((2, 8)), dma((2, 8)), dma((31,)), dma((31,)),
            dma((2, 4)), dma((2, 4)), dma,
        ],
        compiler_params=pltpu.CompilerParams(
            collective_id=0, has_side_effects=True, vmem_limit_bytes=60 * 2**20
        ),
    )(q_nope, q_rope, w_uk, w_uv, w_value.reshape(heads, -1), kv_cache, cutoffs.reshape(rows, 1))
    return attn, value[0]


def solution(mesh):
    placed = (
        P("seq", "head"),
        P("seq", "head"),
        P("head", None, None),
        P("head", None, None),
        P("head"),
        P("seq", None),
        P("seq"),
    )
    return jax.shard_map(
        on_device,
        mesh=mesh,
        in_specs=placed,
        out_specs=(P("seq", "head"), P("seq")),
        check_vma=False,
    )
```

time: 163 us -> 61.2 us (0.38)
  the two profiles are of different devices: /device:TPU:16 before, /device:TPU:1 now
where the time goes in v1:
time: 61.2 us; the launch traced here: 60.5 us
  Pallas kernels  54 us (88%)
  local copies, waits for them, and re-layouts  5.9 us (10%)
  between operations  0.65 us (1%)
    pallas_call x1, Pallas kernels, on_device(): pl.pallas_call(kernel, out_shape=(jax.ShapeDtypeStruct((rows, q_nope.shap...  54 us
    unnamed x4, local copies, waits for them, and re-layouts  3.98 us

profile of v1, /device:TPU:1, one launch (start us, length us, event | category | flops | bytes accessed | tf_op | source)
XLA Modules:
  0.0 60.5 jit_solution(332674579426196381)
XLA Ops:
  0.6 0.0 copy-start
  0.6 0.6 %copy-done = s32[96]{0:T(128)S(1)} copy-done((s32[96]{0:T(128)S(1)}, s32[96]{0:T(128)}, u32[]{:S(2)}) %copy-start) | copy-done | bytes 408
  1.3 0.7 %copy.10.cut = s32[96,1]{1,0:T(8,128)} copy(s32[96,1]{0,1:T(1,128)S(1)} %bitcast.5) | data formatting | bytes 768 | tf_op jit(solution)/shard_map/reshape | solution.py:315
  2.0 1.7 %copy.9.kv = bf16[128,576]{1,0:T(8,128)(2,1)} copy(bf16[128,576]{0,1:T(8,128)(2,1)} %param.12) | data formatting | bytes 294912 | tf_op args[5]
  3.7 54.0 %shard_map.86 = (bf16[96,1024]{1,0:T(8,128)(2,1)}, f32[8,96]{1,0:T(8,128)}) custom-call(bf16[96,1024]{1,0:T(8,128)(2,1)} %qn.1, bf16[96,512]{1,0:T(8,128)(2,1)} %qr.1, bf16[8,128,512]{2,1,0:T(8,128)(2,1)} %w_uk.1, bf16[8,512,128]{2,1,0:T(8,128)(2,1)} %w_uv.1, f32[8,128]{1,0:T(8,128)} %bitcast.4, bf16[128,576]{1,0:T(8,128)(2,1)} %copy.9.kv, s32[96,1]{1,0:T(8,128)} %copy.10.cut), custom_call_target="tpu_custom_call" | custom-call | tf_op jit(solution)/shard_map/pallas_call | solution.py:293
  57.7 1.2 %slice_bitcast_fusion = f32[96]{0:T(128)} fusion(f32[8,96]{1,0:T(8,128)} %get-tuple-element.5), kind=kLoop, calls=%fused_computation | loop fusion | bytes 768 | tf_op jit(solution)/shard_map/squeeze | solution.py:316
  58.9 1.6 %copy.12 = bf16[96,1024]{1,0:T(8,128)(2,1)} copy(bf16[96,1024]{1,0:T(8,128)(2,1)} %get-tuple-element.8) | data formatting | bytes 393216
Async XLA Ops:
  0.6 0.7 %copy-start = (s32[96]{0:T(128)S(1)}, s32[96]{0:T(128)}, u32[]{:S(2)}) copy-start(s32[96]{0:T(128)} %param.13) | copy-start | bytes 1156

commit v2 on v1

--- a/solution.py
+++ b/solution.py
@@ -11,9 +11,8 @@
 HIDDEN = -1e30
 Y, Z_HI, X = 8, 4, 4
 SHARD = 128
-HALF = 64
 CHIP = 2 * SHARD
-BLOCKS = 2
+BLOCKS = 1
 
 
 def chip_slot(plane, away):
@@ -27,9 +26,9 @@
 
 
 def kernel(
-    qn, qr, w_uk, w_uv, w_value, kv, cut, attn, value,
-    held, q_all, accum, top, total, x_sums, z_sums,
-    y_send, y_recv, z_send, z_recv, c_send, c_recv, v_send, v_recv, own_sem,
+    qn_in, qr_in, w_uk_in, w_uv_in, w_value, kv, cut, attn, value,
+    qn, qr, w_uk, w_uv, held, q_all, accum, top, total, x_sums, z_sums,
+    y_send, y_recv, z_send, z_recv, c_send, c_recv, v_send, v_recv, in_sem,
 ):
     rows = qn.shape[0]
     heads, _, latent = w_uk.shape
@@ -57,14 +56,15 @@
     for device in greeted:
         pl.semaphore_signal(barrier, inc=1, device_id=device, device_id_type=MESH)
 
+    part_depth = kv.shape[0] // 2
+
     def place(slot, half=None):
-        start = slot * CHIP + core * SHARD
         if half is None:
-            return held.at[pl.ds(pl.multiple_of(start, SHARD), SHARD)]
-        return held.at[pl.ds(pl.multiple_of(start + half * HALF, HALF), HALF)]
+            return held.at[slot * 2 + core]
+        return held.at[slot * 2 + core, pl.ds(half * part_depth, part_depth)]
 
     def own(half):
-        return kv.at[pl.ds(half * HALF, HALF)]
+        return kv.at[pl.ds(half * part_depth, part_depth)]
 
     def half_of(stream, unit):
         return unit % 2 if stream == 0 else 1 - unit % 2
@@ -141,7 +141,6 @@
         for index in indices:
             twin_copy(index).wait_recv()
 
-    keep_own = pltpu.make_async_copy(kv, place(chip_slot(0, 0)), own_sem)
 
     def first_event(plane, steps):
         z_at = lax.rem(z_lo + plane, 2)
@@ -159,14 +158,12 @@
         size = 2 * CHIP
         column = lax.broadcasted_iota(jnp.int32, (rows, size), 1)
         event = column + jnp.where(column < CHIP, first, second - CHIP)
-        bias = jnp.where(event < cut[...], 0.0, HIDDEN)
-        block = held[pl.ds(pair * size, size), :]
+        bias = jnp.where(event < visible, 0.0, HIDDEN)
+        block = jnp.concatenate([held[pair * 4 + k] for k in range(4)], axis=1)
         per = heads // BLOCKS
         for part in range(BLOCKS):
             span = pl.ds(part * per * rows, per * rows)
-            score = lax.dot_general(
-                q_all[span, :], block, (((1,), (1,)), ((), ())), preferred_element_type=jnp.float32
-            )
+            score = jnp.dot(q_all[span, :], block, preferred_element_type=jnp.float32)
             weights, scales = [], []
             for h in range(per):
                 mine = pl.ds((part * per + h) * rows, rows)
@@ -181,19 +178,27 @@
                 total[mine, :] = added if pair == 0 else total[mine, :] * scale + added
                 top[mine, :] = jnp.broadcast_to(newest, (rows, 128))
                 weights.append(w.astype(jnp.bfloat16))
-            update = jnp.dot(
-                jnp.concatenate(weights, axis=0), block[:, :latent], preferred_element_type=jnp.float32
+            update = lax.dot_general(
+                jnp.concatenate(weights, axis=0), block[:latent], (((1,), (1,)), ((), ())),
+                preferred_element_type=jnp.float32,
             )
             if pair == 0:
                 accum[span, :] = update
             else:
                 accum[span, :] = accum[span, :] * jnp.concatenate(scales, axis=0) + update
 
-    for h in range(heads):
-        mine = pl.ds(h * rows, rows)
-        q_lat = jnp.dot(qn[:, h * 128 : (h + 1) * 128], w_uk[h], preferred_element_type=jnp.float32)
-        q_all[mine, :latent] = q_lat.astype(jnp.bfloat16)
-        q_all[mine, latent:] = qr[:, h * rope : (h + 1) * rope]
+    fetches = [
+        pltpu.make_async_copy(source, target, in_sem.at[k])
+        for k, (source, target) in enumerate(
+            ((qn_in, qn), (w_uk_in, w_uk), (qr_in, qr), (kv, place(chip_slot(0, 0))), (w_uv_in, w_uv))
+        )
+    ]
+    for fetch in fetches:
+        fetch.start()
+    square = (rows, rows)
+    on_diagonal = lax.broadcasted_iota(jnp.int32, square, 0) == lax.broadcasted_iota(jnp.int32, square, 1)
+    as_row = jnp.broadcast_to(cut[...].astype(jnp.float32), square)
+    visible = jnp.sum(jnp.where(on_diagonal, as_row, 0.0), axis=1, keepdims=True).astype(jnp.int32)
 
     pl.semaphore_wait(barrier, len(greeted))
     for unit in range(2):
@@ -202,12 +207,19 @@
             if unit == 0:
                 z_copy(stream, 0).start()
     twin_copy(0).start()
-    keep_own.start()
+
+    for fetch in fetches[:3]:
+        fetch.wait()
+    for h in range(heads):
+        mine = pl.ds(h * rows, rows)
+        q_lat = jnp.dot(qn[:, h * 128 : (h + 1) * 128], w_uk[h], preferred_element_type=jnp.float32)
+        q_all[mine, :latent] = q_lat.astype(jnp.bfloat16)
+        q_all[mine, latent:] = qr[:, h * rope : (h + 1) * rope]
 
     from_y(0)
     from_z(0)
     from_y(1)
-    keep_own.wait()
+    fetches[3].wait()
     from_twin(0, 15, 16)
     attend(0)
     from_y(2)
@@ -237,6 +249,7 @@
     from_twin(13, 14, 29, 30)
     attend(7)
 
+    fetches[4].wait()
     share = jnp.zeros((rows, 128), jnp.float32)
     for h in range(heads):
         mine = pl.ds(h * rows, rows)
@@ -273,7 +286,7 @@
         return result
 
     along_x = exchange(0, x_sums, x_peers, x, X, partial)
-    value[...] = exchange(1, z_sums, z_peers, z_hi, Z_HI, along_x)
+    value[...] = exchange(1, z_sums, z_peers, z_hi, Z_HI, along_x)[:1]
 
     for stream in range(2):
         for unit in range(7):
@@ -288,18 +301,23 @@
     rows = q_nope.shape[0]
     heads, _, latent = w_uk.shape
     depth = kv_cache.shape[1]
+    place = pl.BlockSpec(memory_space=pl.ANY)
     vmem = pl.BlockSpec(memory_space=pltpu.VMEM)
     dma = pltpu.SemaphoreType.DMA
     attn, value = pl.pallas_call(
         kernel,
         out_shape=(
             jax.ShapeDtypeStruct((rows, q_nope.shape[1]), jnp.bfloat16),
-            jax.ShapeDtypeStruct((8, rows), jnp.float32),
+            jax.ShapeDtypeStruct((1, rows), jnp.float32),
         ),
-        in_specs=[vmem] * 7,
+        in_specs=[place] * 4 + [vmem, place, vmem],
         out_specs=(vmem, vmem),
         scratch_shapes=[
-            pltpu.VMEM((16 * CHIP, depth), jnp.bfloat16),
+            pltpu.VMEM(q_nope.shape, jnp.bfloat16),
+            pltpu.VMEM(q_rope.shape, jnp.bfloat16),
+            pltpu.VMEM(w_uk.shape, jnp.bfloat16),
+            pltpu.VMEM(w_uv.shape, jnp.bfloat16),
+            pltpu.VMEM((32, depth, SHARD), jnp.bfloat16),
             pltpu.VMEM((heads * rows, depth), jnp.bfloat16),
             pltpu.VMEM((heads * rows, latent), jnp.float32),
             pltpu.VMEM((heads * rows, 128), jnp.float32),
@@ -307,13 +325,13 @@
             pltpu.VMEM((X, 8, 128), jnp.float32),
             pltpu.VMEM((Z_HI, 8, 128), jnp.float32),
             dma((2, 7)), dma((2, 7)), dma((2, 8)), dma((2, 8)), dma((31,)), dma((31,)),
-            dma((2, 4)), dma((2, 4)), dma,
+            dma((2, 4)), dma((2, 4)), dma((5,)),
         ],
         compiler_params=pltpu.CompilerParams(
             collective_id=0, has_side_effects=True, vmem_limit_bytes=60 * 2**20
         ),
-    )(q_nope, q_rope, w_uk, w_uv, w_value.reshape(heads, -1), kv_cache, cutoffs.reshape(rows, 1))
-    return attn, value[0]
+    )(q_nope, q_rope, w_uk, w_uv, w_value.reshape(heads, -1), kv_cache.T, cutoffs.reshape(1, rows))
+    return attn, value.reshape(rows)
 
 
 def solution(mesh):

time: 61.2 us -> 55 us (0.90)
  local copies, waits for them, and re-layouts: 5.9 us -> 2.13 us
  Pallas kernels: 54 us -> 51.7 us
    pallas_call x1, Pallas kernels: 54 us -> 51.7 us  [on_device(): pl.pallas_call(kernel, out_shape=(jax.ShapeDtypeStruct((rows, q_nope.shap...]
    unnamed x4, local copies, waits for them, and re-layouts: 3.98 us -> 2.13 us
    squeeze x1 -> x0, local copies, waits for them, and re-layouts: 1.2 us -> none  [on_device(): return (attn, value[0])]
    reshape x1 -> x0, local copies, waits for them, and re-layouts: 0.73 us -> none  [on_device(): cutoffs.reshape(rows, 1)]
where the time goes in v2:
time: 55 us; the launch traced here: 54.5 us
  Pallas kernels  51.7 us (94%)
  local copies, waits for them, and re-layouts  2.13 us (4%)
  between operations  0.65 us (1%)
    pallas_call x1, Pallas kernels, on_device(): pl.pallas_call(kernel, out_shape=(jax.ShapeDtypeStruct((rows, q_nope.shap...  51.7 us
    unnamed x4, local copies, waits for them, and re-layouts  2.13 us

profile of v2, /device:TPU:1, one launch (start us, length us, event | category | flops | bytes accessed | tf_op | source)
XLA Modules:
  0.0 54.5 jit_solution(288585399985807470)
XLA Ops:
  0.6 51.7 %shard_map.86 = (bf16[96,1024]{1,0:T(8,128)(2,1)}, f32[1,96]{1,0:T(1,128)}) custom-call(bf16[96,1024]{1,0:T(8,128)(2,1)} %qn_in.1, bf16[96,512]{1,0:T(8,128)(2,1)} %qr_in.1, bf16[8,128,512]{2,1,0:T(8,128)(2,1)} %w_uk_in.1, bf16[8,512,128]{2,1,0:T(8,128)(2,1)} %w_uv_in.1, f32[8,128]{1,0:T(8,128)} %bitcast.5, bf16[576,128]{1,0:T(8,128)(2,1)} %bitcast.4, ...), custom_call_target="tpu_custom_call" | custom-call | tf_op jit(solution)/shard_map/pallas_call | solution.py:307
  52.3 0.0 copy-start
  52.3 1.6 %copy.11 = bf16[96,1024]{1,0:T(8,128)(2,1)} copy(bf16[96,1024]{1,0:T(8,128)(2,1)} %get-tuple-element.8) | data formatting | bytes 393216
  54.0 0.0 copy-done
  54.0 0.5 copy.12
Async XLA Ops:
  52.3 1.6 %copy-start = (f32[1,96]{1,0:T(1,128)S(1)}, f32[1,96]{1,0:T(1,128)}, u32[]{:S(2)}) copy-start(f32[1,96]{1,0:T(1,128)} %get-tuple-element.5) | copy-start | bytes 1156

commit v3 on v2

--- a/solution.py
+++ b/solution.py
@@ -28,7 +28,7 @@
 def kernel(
     qn_in, qr_in, w_uk_in, w_uv_in, w_value, kv, cut, attn, value,
     qn, qr, w_uk, w_uv, held, q_all, accum, top, total, x_sums, z_sums,
-    y_send, y_recv, z_send, z_recv, c_send, c_recv, v_send, v_recv, in_sem,
+    y_send, y_recv, z_send, z_recv, x_send, x_recv, c_send, c_recv, v_send, v_recv, in_sem,
 ):
     rows = qn.shape[0]
     heads, _, latent = w_uk.shape
@@ -56,15 +56,21 @@
     for device in greeted:
         pl.semaphore_signal(barrier, inc=1, device_id=device, device_id_type=MESH)
 
-    part_depth = kv.shape[0] // 2
-
-    def place(slot, half=None):
-        if half is None:
+    third = kv.shape[0] // 3
+    odd = lax.rem(x, 2)
+    piece_at = (0, third * (1 + odd), third * (2 - odd))
+
+    def rows_of(piece):
+        start = piece_at[piece]
+        return pl.ds(start if piece == 0 else pl.multiple_of(start, third), third)
+
+    def place(slot, piece=None):
+        if piece is None:
             return held.at[slot * 2 + core]
-        return held.at[slot * 2 + core, pl.ds(half * part_depth, part_depth)]
-
-    def own(half):
-        return kv.at[pl.ds(half * part_depth, part_depth)]
+        return held.at[slot * 2 + core, rows_of(piece)]
+
+    def own(piece):
+        return kv.at[rows_of(piece)]
 
     def half_of(stream, unit):
         return unit % 2 if stream == 0 else 1 - unit % 2
@@ -100,9 +106,29 @@
             device_id_type=MESH,
         )
 
+    def x_slot(index):
+        unit = index if index < 7 else index - 8
+        if unit < 0:
+            return chip_slot(1, 0), 1
+        stream, steps = (0 if unit % 2 else 1), unit // 2 + 1
+        return chip_slot(index // 7 if index < 14 else 1, away(stream, steps)), 1 if stream == 1 and steps < 4 else 0
+
+    def x_copy(index):
+        slot, down = x_slot(index)
+        return pltpu.make_async_remote_copy(
+            src_ref=place(slot, 1),
+            dst_ref=place(slot, 1),
+            send_sem=x_send.at[index],
+            recv_sem=x_recv.at[index],
+            device_id=x_peers[X - 2 if down else 0],
+            device_id_type=MESH,
+        )
+
     def twin_copy(index):
         if index == 0:
             source, target = kv, place(chip_slot(0, 0))
+        elif index > 30:
+            source = target = place(x_slot(index - 31)[0], 2)
         else:
             if index < 15:
                 stream, unit = (index - 1) % 2, (index - 1) // 2
@@ -131,11 +157,20 @@
                 y_copy(stream, unit + 2).start()
             z_copy(stream, unit + 1).start()
             twin_copy(1 + unit * 2 + stream).start()
+            if half_of(stream, unit) == 1:
+                x_copy(unit).start()
 
     def from_z(unit):
         for stream in range(2):
             z_copy(stream, unit).wait_recv()
             twin_copy(15 + unit * 2 + stream).start()
+            if (stream if unit == 0 else half_of(stream, unit - 1)) == 1:
+                x_copy(7 + unit).start()
+
+    def from_x(*indices):
+        for index in indices:
+            x_copy(index).wait_recv()
+            twin_copy(31 + index).start()
 
     def from_twin(*indices):
         for index in indices:
@@ -219,34 +254,41 @@
     from_y(0)
     from_z(0)
     from_y(1)
+    from_z(1)
     fetches[3].wait()
-    from_twin(0, 15, 16)
+    from_x(7)
+    from_twin(0, 15, 16, 38)
     attend(0)
     from_y(2)
-    from_z(1)
     from_z(2)
-    from_twin(1, 2, 3, 4)
+    from_x(0, 1)
+    from_y(3)
+    from_twin(1, 2, 3, 4, 31, 32)
     attend(1)
-    from_y(3)
-    from_twin(17, 18, 19, 20)
+    from_z(3)
+    from_x(8, 9)
+    from_y(4)
+    from_twin(17, 18, 19, 20, 39, 40)
     attend(2)
-    from_y(4)
-    from_z(3)
+    from_y(5)
     from_z(4)
-    from_twin(5, 6, 7, 8)
+    from_x(2, 3)
+    from_twin(5, 6, 7, 8, 33, 34)
     attend(3)
-    from_y(5)
-    from_twin(21, 22, 23, 24)
-    attend(4)
     from_y(6)
     from_z(5)
+    from_x(10, 11)
+    from_twin(21, 22, 23, 24, 41, 42)
+    attend(4)
     from_z(6)
-    from_twin(9, 10, 11, 12)
+    from_z(7)
+    from_x(4, 5)
+    from_twin(9, 10, 11, 12, 35, 36)
     attend(5)
-    from_z(7)
-    from_twin(25, 26, 27, 28)
+    from_x(12, 13, 6, 14)
+    from_twin(25, 26, 27, 28, 43, 44)
     attend(6)
-    from_twin(13, 14, 29, 30)
+    from_twin(13, 14, 29, 30, 37, 45)
     attend(7)
 
     fetches[4].wait()
@@ -293,7 +335,9 @@
             y_copy(stream, unit).wait_send()
         for unit in range(8):
             z_copy(stream, unit).wait_send()
-    for index in range(31):
+    for index in range(15):
+        x_copy(index).wait_send()
+    for index in range(46):
         twin_copy(index).wait_send()
 
 
@@ -324,7 +368,7 @@
             pltpu.VMEM((heads * rows, 128), jnp.float32),
             pltpu.VMEM((X, 8, 128), jnp.float32),
             pltpu.VMEM((Z_HI, 8, 128), jnp.float32),
-            dma((2, 7)), dma((2, 7)), dma((2, 8)), dma((2, 8)), dma((31,)), dma((31,)),
+            dma((2, 7)), dma((2, 7)), dma((2, 8)), dma((2, 8)), dma((15,)), dma((15,)), dma((46,)), dma((46,)),
             dma((2, 4)), dma((2, 4)), dma((5,)),
         ],
         compiler_params=pltpu.CompilerParams(

time: 55 us -> 60.3 us (1.096)
  Pallas kernels: 51.7 us -> 57.3 us
    pallas_call x1, Pallas kernels: 51.7 us -> 57.3 us  [on_device(): pl.pallas_call(kernel, out_shape=(jax.ShapeDtypeStruct((rows, q_nope.shap...]
where the time goes in v3:
time: 60.3 us; the launch traced here: 60.1 us
  Pallas kernels  57.3 us (95%)
  local copies, waits for them, and re-layouts  2.13 us (4%)
  between operations  0.65 us (1%)
    pallas_call x1, Pallas kernels, on_device(): pl.pallas_call(kernel, out_shape=(jax.ShapeDtypeStruct((rows, q_nope.shap...  57.3 us
    unnamed x4, local copies, waits for them, and re-layouts  2.13 us

profile of v3, /device:TPU:1, one launch (start us, length us, event | category | flops | bytes accessed | tf_op | source)
XLA Modules:
  0.0 60.1 jit_solution(12555214477807711200)
XLA Ops:
  0.6 57.3 %shard_map.86 = (bf16[96,1024]{1,0:T(8,128)(2,1)}, f32[1,96]{1,0:T(1,128)}) custom-call(bf16[96,1024]{1,0:T(8,128)(2,1)} %qn_in.1, bf16[96,512]{1,0:T(8,128)(2,1)} %qr_in.1, bf16[8,128,512]{2,1,0:T(8,128)(2,1)} %w_uk_in.1, bf16[8,512,128]{2,1,0:T(8,128)(2,1)} %w_uv_in.1, f32[8,128]{1,0:T(8,128)} %bitcast.5, bf16[576,128]{1,0:T(8,128)(2,1)} %bitcast.4, ...), custom_call_target="tpu_custom_call" | custom-call | tf_op jit(solution)/shard_map/pallas_call | solution.py:351
  58.0 0.0 copy-start
  58.0 1.6 %copy.11 = bf16[96,1024]{1,0:T(8,128)(2,1)} copy(bf16[96,1024]{1,0:T(8,128)(2,1)} %get-tuple-element.8) | data formatting | bytes 393216
  59.6 0.0 copy-done
  59.6 0.5 copy.12
Async XLA Ops:
  58.0 1.6 %copy-start = (f32[1,96]{1,0:T(1,128)S(1)}, f32[1,96]{1,0:T(1,128)}, u32[]{:S(2)}) copy-start(f32[1,96]{1,0:T(1,128)} %get-tuple-element.5) | copy-start | bytes 1156

commit v4 on v2

--- a/solution.py
+++ b/solution.py
@@ -52,7 +52,8 @@
     z_peers = [(seq, x * Z_HI + lax.rem(z_hi + k, Z_HI)) for k in range(1, Z_HI)]
 
     barrier = pltpu.get_barrier_semaphore()
-    greeted = [*y_to, *z_to, twin, *x_peers, *z_peers]
+    hand_to = (twin, (twin[0], x_peers[0][1]), twin, (twin[0], x_peers[X - 2][1]))
+    greeted = [*y_to, *z_to, *hand_to[1:], *x_peers, *z_peers]
     for device in greeted:
         pl.semaphore_signal(barrier, inc=1, device_id=device, device_id_type=MESH)
 
@@ -120,7 +121,7 @@
             dst_ref=target,
             send_sem=c_send.at[index],
             recv_sem=c_recv.at[index],
-            device_id=twin,
+            device_id=hand_to[index % 4],
             device_id_type=MESH,
         )
 

time: 55 us -> 60.6 us (1.10)
  Pallas kernels: 51.7 us -> 57.6 us
    pallas_call x1, Pallas kernels: 51.7 us -> 57.6 us  [on_device(): pl.pallas_call(kernel, out_shape=(jax.ShapeDtypeStruct((rows, q_nope.shap...]
where the time goes in v4:
time: 60.6 us; the launch traced here: 60.4 us
  Pallas kernels  57.6 us (95%)
  local copies, waits for them, and re-layouts  2.13 us (4%)
  between operations  0.65 us (1%)
    pallas_call x1, Pallas kernels, on_device(): pl.pallas_call(kernel, out_shape=(jax.ShapeDtypeStruct((rows, q_nope.shap...  57.6 us
    unnamed x4, local copies, waits for them, and re-layouts  2.13 us

profile of v4, /device:TPU:1, one launch (start us, length us, event | category | flops | bytes accessed | tf_op | source)
XLA Modules:
  0.0 60.4 jit_solution(3514988531751140678)
XLA Ops:
  0.6 57.6 %shard_map.86 = (bf16[96,1024]{1,0:T(8,128)(2,1)}, f32[1,96]{1,0:T(1,128)}) custom-call(bf16[96,1024]{1,0:T(8,128)(2,1)} %qn_in.1, bf16[96,512]{1,0:T(8,128)(2,1)} %qr_in.1, bf16[8,128,512]{2,1,0:T(8,128)(2,1)} %w_uk_in.1, bf16[8,512,128]{2,1,0:T(8,128)(2,1)} %w_uv_in.1, f32[8,128]{1,0:T(8,128)} %bitcast.5, bf16[576,128]{1,0:T(8,128)(2,1)} %bitcast.4, ...), custom_call_target="tpu_custom_call" | custom-call | tf_op jit(solution)/shard_map/pallas_call | solution.py:308
  58.2 0.0 copy-start
  58.3 1.6 %copy.11 = bf16[96,1024]{1,0:T(8,128)(2,1)} copy(bf16[96,1024]{1,0:T(8,128)(2,1)} %get-tuple-element.8) | data formatting | bytes 393216
  59.9 0.0 copy-done
  59.9 0.5 copy.12
Async XLA Ops:
  58.2 1.6 %copy-start = (f32[1,96]{1,0:T(1,128)S(1)}, f32[1,96]{1,0:T(1,128)}, u32[]{:S(2)}) copy-start(f32[1,96]{1,0:T(1,128)} %get-tuple-element.5) | copy-start | bytes 1156
